TPU v7x, 32 devices: a whole 2x2x4 slice. The times are simulated.
32 devices in a mesh: section: 4 (over y, x), dp: 2 (over core), tensor: 4 (over z).
Axes of the slice: x: 2, y: 2, z: 4, core: 2. Of those that a mesh axis runs over, the one named last changes fastest.
Arguments:
- cotangent: bfloat16 [2, 256, 8192], P(None, 'dp', 'tensor'), may hold values from -6 to 6
- stash: bfloat16 [4, 2, 256, 8192], P('section', None, 'dp', 'tensor'), may hold values from -0.25 to 0.25
- factor_a: bfloat16 [4, 1024, 8192], P('section', 'dp', 'tensor'), may hold values from -0.0625 to 0.0625
- factor_b: bfloat16 [4, 8192, 1024], P('section', ('tensor', 'dp')), may hold values from -0.1875 to 0.1875
- block_vals: bfloat16 [4, 8, 128, 128], P('section', ('dp', 'tensor')), may hold values from -0.25 to 0.25
- block_rows: int32 [4, 8], P('section'), may hold values from 0 to 63, as said below
- block_cols: int32 [4, 8], P('section'), may hold values from 0 to 63, as said below
Outputs:
- grad_in: bfloat16 [4, 2, 256, 8192], P('section', None, 'dp', 'tensor')
- block_grad: float32 [4, 8, 128, 128], P('section', ('dp', 'tensor'))
Inputs may be any that keep to these rules, and one draw needn't show every extreme that they name: The support lies inside the diagonal part of each tensor shard. Within a section all (block_rows, block_cols) pairs are distinct. For every dp index o < 2, tensor index t < 4 and slot k < 1, the block at position (o * 4 + t) + k has both its row and its column block index in [t * 8192 // (128 * 4), (t + 1) * 8192 // (128 * 4)). `block_cols`: drawn together with block_rows; the same promise holds.
All inputs are finite; a program needn't handle non-finite values.
Results may differ from a plain program's by a relative error of at most 0.024.
Values may be sent and summed in bfloat16 or wider, within the bound.
A program may use at most 128 MiB of HBM per device.

v0:
```python
import jax
import jax.numpy as jnp
from jax import lax
from jax.sharding import PartitionSpec as P


def shifted(value, axis, steps):
    count = lax.axis_size(axis)
    initial, last = (max(0, -steps), min(count, count - steps))
    return lax.ppermute(value, axis, [(source, source + steps) for source in range(initial, last)])


def pass_back(grad_out):
    return shifted(grad_out, "section", -1)


def on_device(cotangent, stash, factor_a, factor_b, block_vals, block_rows, block_cols):
    sections = lax.axis_size("section")
    section_pos = lax.axis_index("section")
    tensor_pos = lax.axis_index("tensor")
    dp_count = lax.axis_size("dp")
    tensor_count = lax.axis_size("tensor")
    left_full, right_full, values = (
        lax.all_gather(factor_a[0], "dp", axis=0, tiled=True),
        lax.all_gather(factor_b[0], "dp", axis=0, tiled=True),
        lax.all_gather(block_vals[0], "dp", axis=0, tiled=True),
    )
    batches = stash.shape[1]
    tokens_here = stash.shape[2]
    local_width = stash.shape[3]
    block_size = block_vals.shape[-1]
    local_blocks = local_width // block_size

    def local_ids(table):
        grid = table[0].reshape(dp_count, tensor_count, -1)
        mine = lax.dynamic_index_in_dim(grid, tensor_pos, 1, keepdims=False)
        return mine.reshape(-1) - tensor_pos * local_blocks

    positions = jnp.arange(local_blocks, dtype=jnp.int32)[None, :]
    row_hits = local_ids(block_rows)[:, None] == positions
    col_hits = local_ids(block_cols)[:, None] == positions
    row_pick = row_hits.astype(jnp.bfloat16)
    row_double = jnp.concatenate([row_pick, row_pick], axis=0)
    col_pick = col_hits.astype(jnp.bfloat16)
    grad_sum = jnp.zeros((values.shape[0], block_size, block_size), jnp.float32)
    grads_in = jnp.zeros(stash.shape[1:], jnp.bfloat16)
    received = jnp.zeros((tokens_here, local_width), jnp.bfloat16)
    steps = batches + sections - 1
    for step_idx in range(steps):
        batch_pos = step_idx - (sections - 1 - section_pos)
        active = (batch_pos >= 0) & (batch_pos < batches)
        slot_pos = jnp.clip(batch_pos, 0, batches - 1)
        fresh = lax.dynamic_index_in_dim(cotangent, slot_pos, 0, keepdims=False)
        cot_now = jnp.where(section_pos == sections - 1, fresh, received)
        partial_value = jnp.einsum(
            "td,rd->tr", cot_now, left_full, preferred_element_type=jnp.float32
        )
        share = lax.psum_scatter(
            partial_value.astype(jnp.bfloat16), "tensor", scatter_dimension=1, tiled=True
        )
        rank_act = lax.all_gather(share, "tensor", axis=1, tiled=True)
        picked_cot = jnp.einsum(
            "tlc,nl->tnc",
            cot_now.reshape(tokens_here, local_blocks, block_size),
            col_pick,
            preferred_element_type=jnp.float32,
        ).astype(jnp.bfloat16)
        sparse_terms = jnp.einsum(
            "tnc,nrc->tnr", picked_cot, values, preferred_element_type=jnp.float32
        )
        upper_part = sparse_terms.astype(jnp.bfloat16)
        lower_part = (sparse_terms - upper_part.astype(jnp.float32)).astype(jnp.bfloat16)
        both_parts = jnp.concatenate([upper_part, lower_part], axis=1)
        sparse_grad = jnp.einsum(
            "tnr,nl->tlr", both_parts, row_double, preferred_element_type=jnp.float32
        )
        dense_grad = jnp.einsum(
            "tr,dr->td", rank_act, right_full, preferred_element_type=jnp.float32
        )
        grad_out = (dense_grad + sparse_grad.reshape(tokens_here, local_width)).astype(jnp.bfloat16)
        current = lax.dynamic_index_in_dim(grads_in, slot_pos, 0, keepdims=False)
        grads_in = lax.dynamic_update_index_in_dim(
            grads_in, jnp.where(active, grad_out, current), slot_pos, 0
        )
        stash_now = lax.dynamic_index_in_dim(stash[0], slot_pos, 0, keepdims=False)
        live_scale = active.astype(jnp.bfloat16)
        if step_idx + 1 < steps:
            received = pass_back(grad_out)
        picked_in = (
            jnp.einsum(
                "tlr,nl->tnr",
                stash_now.reshape(tokens_here, local_blocks, block_size),
                row_pick,
                preferred_element_type=jnp.float32,
            ).astype(jnp.bfloat16)
            * live_scale
        )
        grad_sum = grad_sum + jnp.einsum(
            "tnr,tnc->nrc", picked_in, picked_cot, preferred_element_type=jnp.float32
        )
    block_grad = lax.psum_scatter(
        grad_sum.astype(jnp.bfloat16), "dp", scatter_dimension=0, tiled=True
    ).astype(jnp.float32)
    return (grads_in[None], block_grad[None])


def solution(mesh):
    in_specs = (
        P(None, "dp", "tensor"),
        P("section", None, "dp", "tensor"),
        P("section", "dp", "tensor"),
        P("section", ("tensor", "dp"), None),
        P("section", ("dp", "tensor"), None, None),
        P("section", None),
        P("section", None),
    )
    out_specs = (P("section", None, "dp", "tensor"), P("section", ("dp", "tensor"), None, None))
    return jax.shard_map(
        on_device, mesh=mesh, in_specs=in_specs, out_specs=out_specs, check_vma=False
    )
```

profile of v0, /device:TPU:0, one launch (start us, length us, event | category | flops | bytes accessed | tf_op | source)
XLA Modules:
  0.0 300.2 jit_solution(10202126768568250833)
XLA Ops:
  8.0 17.9 %all-gather.6.cloned.1.call-done = bf16[1,1024,2048]{2,1,0:T(8,128)(2,1)} async-done(((bf16[1,512,2048]{2,1,0:T(8,128)(2,1)}), bf16[1,1024,2048]{2,1,0:T(8,128)(2,1)}) %all-gather.6.cloned.1.call-update) | async-done | bytes 4194320 | tf_op jit(solution)/shard_map/all_gather | solution.py:24
  25.9 4.6 %fusion.59 = bf16[128,1024]{1,0:T(8,128)(2,1)} fusion(bf16[1,1024,2048]{2,1,0:T(8,128)(2,1)} %all-gather.6.cloned.1.call-done, bf16[2,128,2048]{2,1,0:T(8,128)(2,1)} %param.7, s32[]{:T(128)S(6)} %min.16, pred[]{:T(512)S(6)} %eq.14), kind=kOutput, calls=%fused_computation.33 | convolution fusion | flops 537264128 | bytes 4980741 | tf_op jit(solution)/shard_map/td,rd->tr/dot_general | solution.py:55
  33.6 1.5 dynamic-slice_bitcast_fusion
  35.0 0.9 copy.71
  36.2 1.9 all-gather.2
  39.0 12.9 %reduce-scatter.7.cloned.1.call-done = bf16[128,256]{1,0:T(8,128)(2,1)} async-done(((bf16[128,1024]{1,0:T(8,128)(2,1)}), bf16[128,256]{1,0:T(8,128)(2,1)}) %reduce-scatter.7.cloned.1.call-update) | async-done | bytes 65552 | tf_op jit(solution)/shard_map/reduce_scatter | solution.py:58
  51.9 14.0 %all_gather.25 = bf16[128,1024]{1,0:T(8,128)(2,1)S(1)} all-gather(bf16[128,256]{1,0:T(8,128)(2,1)} %reduce-scatter.7.cloned.1.call-done), channel_id=1, replica_groups=mesh['section'=4,'dp'=2,'tensor'=4] {'tensor'}, dimensions={1}, use_global_device_ids=true | all-gather | bytes 327680 | tf_op jit(solution)/shard_map/all_gather | solution.py:61
  66.0 4.7 %bitcast_dynamic-update-slice_fusion.3 = (bf16[2,128,2048]{2,1,0:T(8,128)(2,1)S(1)}, bf16[128,2048]{1,0:T(8,128)(2,1)}) fusion(bf16[2,128,2048]{2,1,0:T(8,128)(2,1)S(1)} %broadcast_in_dim.36, s32[]{:T(128)S(6)} %min.16, pred[]{:T(512)S(6)} %and.17, f32[16,8,16,128]{3,2,1,0:T(8,128)S(1)} %bitcast.277, bf16[128,1024]{1,0:T(8,128)(2,1)S(1)} %all_gather.25, ...), kind=kOutput, calls=%fused_computation.83 | convolution fusion | flops 537657344 | bytes 6553605 | tf_op jit(solution)/shard_map/tr,dr->td/dot_general | solution.py:77
  70.7 1.3 collective-permute-start
  72.0 2.0 fusion.81
  74.0 1.1 copy.72
  75.1 2.0 copy.73
  77.1 0.9 fusion.83
  78.0 0.8 constant_dynamic-slice_fusion.2
  78.8 7.5 %collective-permute-done = bf16[128,2048]{1,0:T(8,128)(2,1)S(1)} collective-permute-done((bf16[128,2048]{1,0:T(8,128)(2,1)}, bf16[128,2048]{1,0:T(8,128)(2,1)S(1)}, u32[]{:S(2)}, u32[]{:S(2)}) %collective-permute-start) | collective-permute-done | bytes 524320 | tf_op jit(solution)/shard_map/ppermute | solution.py:10
  86.8 2.2 fusion.62
  89.8 20.7 %reduce-scatter.9.cloned.1.call-done = bf16[128,256]{1,0:T(8,128)(2,1)} async-done(((bf16[128,1024]{1,0:T(8,128)(2,1)}), bf16[128,256]{1,0:T(8,128)(2,1)}) %reduce-scatter.9.cloned.1.call-update) | async-done | bytes 65552 | tf_op jit(solution)/shard_map/reduce_scatter | solution.py:58
  110.4 14.2 %all_gather.28 = bf16[128,1024]{1,0:T(8,128)(2,1)S(1)} all-gather(bf16[128,256]{1,0:T(8,128)(2,1)} %reduce-scatter.9.cloned.1.call-done), channel_id=1, replica_groups=mesh['section'=4,'dp'=2,'tensor'=4] {'tensor'}, dimensions={1}, use_global_device_ids=true | all-gather | bytes 327680 | tf_op jit(solution)/shard_map/all_gather | solution.py:61
  124.6 4.8 %bitcast_dynamic-update-slice_fusion.2 = (bf16[2,128,2048]{2,1,0:T(8,128)(2,1)S(1)}, bf16[128,2048]{1,0:T(8,128)(2,1)}) fusion(bf16[2,128,2048]{2,1,0:T(8,128)(2,1)S(1)} %get-tuple-element.17, s32[]{:T(128)S(6)} %min.17, bf16[1,128,2048]{2,1,0:T(8,128)(2,1)} %constant_dynamic-slice_fusion.2, pred[]{:T(512)S(6)} %and.18, ...), kind=kOutput, calls=%fused_computation.80 | convolution fusion | flops 537657344 | bytes 7077893 | tf_op jit(solution)/shard_map/tr,dr->td/dot_general | solution.py:77
  129.4 1.3 collective-permute-start.1
  130.7 0.9 fusion.85
  131.6 1.1 copy.74
  132.8 0.9 fusion.87
  134.6 6.4 %collective-permute-done.1 = bf16[128,2048]{1,0:T(8,128)(2,1)S(1)} collective-permute-done((bf16[128,2048]{1,0:T(8,128)(2,1)}, bf16[128,2048]{1,0:T(8,128)(2,1)S(1)}, u32[]{:S(2)}, u32[]{:S(2)}) %collective-permute-start.1) | collective-permute-done | bytes 524320 | tf_op jit(solution)/shard_map/ppermute | solution.py:10
  141.4 2.2 fusion.65
  144.4 17.8 %reduce-scatter.11.cloned.1.call-done = bf16[128,256]{1,0:T(8,128)(2,1)} async-done(((bf16[128,1024]{1,0:T(8,128)(2,1)}), bf16[128,256]{1,0:T(8,128)(2,1)}) %reduce-scatter.11.cloned.1.call-update) | async-done | bytes 65552 | tf_op jit(solution)/shard_map/reduce_scatter | solution.py:58
  162.2 14.4 %all_gather.29 = bf16[128,1024]{1,0:T(8,128)(2,1)S(1)} all-gather(bf16[128,256]{1,0:T(8,128)(2,1)} %reduce-scatter.11.cloned.1.call-done), channel_id=1, replica_groups=mesh['section'=4,'dp'=2,'tensor'=4] {'tensor'}, dimensions={1}, use_global_device_ids=true | all-gather | bytes 327680 | tf_op jit(solution)/shard_map/all_gather | solution.py:61
  176.6 4.8 %bitcast_dynamic-update-slice_fusion.1 = (bf16[2,128,2048]{2,1,0:T(8,128)(2,1)S(1)}, bf16[128,2048]{1,0:T(8,128)(2,1)}) fusion(bf16[2,128,2048]{2,1,0:T(8,128)(2,1)S(1)} %get-tuple-element.19, s32[]{:T(128)S(6)} %min.18, bf16[1,128,2048]{2,1,0:T(8,128)(2,1)} %constant_dynamic-slice_fusion.1, pred[]{:T(512)S(6)} %and.19, ...), kind=kOutput, calls=%fused_computation.77 | convolution fusion | flops 537657344 | bytes 7077893 | tf_op jit(solution)/shard_map/tr,dr->td/dot_general | solution.py:77
  181.4 1.3 collective-permute-start.2
  182.7 0.9 fusion.116
  183.6 1.1 copy.75
  184.7 0.9 fusion.89
  185.6 0.9 constant_dynamic-slice_fusion
  186.6 6.2 %collective-permute-done.2 = bf16[128,2048]{1,0:T(8,128)(2,1)S(1)} collective-permute-done((bf16[128,2048]{1,0:T(8,128)(2,1)}, bf16[128,2048]{1,0:T(8,128)(2,1)S(1)}, u32[]{:S(2)}, u32[]{:S(2)}) %collective-permute-start.2) | collective-permute-done | bytes 524320 | tf_op jit(solution)/shard_map/ppermute | solution.py:10
  193.2 2.2 fusion.68
  196.2 17.9 %reduce-scatter.13.cloned.1.call-done = bf16[128,256]{1,0:T(8,128)(2,1)} async-done(((bf16[128,1024]{1,0:T(8,128)(2,1)}), bf16[128,256]{1,0:T(8,128)(2,1)}) %reduce-scatter.13.cloned.1.call-update) | async-done | bytes 65552 | tf_op jit(solution)/shard_map/reduce_scatter | solution.py:58
  214.0 14.2 %all_gather.30 = bf16[128,1024]{1,0:T(8,128)(2,1)S(1)} all-gather(bf16[128,256]{1,0:T(8,128)(2,1)} %reduce-scatter.13.cloned.1.call-done), channel_id=1, replica_groups=mesh['section'=4,'dp'=2,'tensor'=4] {'tensor'}, dimensions={1}, use_global_device_ids=true | all-gather | bytes 327680 | tf_op jit(solution)/shard_map/all_gather | solution.py:61
  228.2 4.0 %bitcast_dynamic-update-slice_fusion = (bf16[2,128,2048]{2,1,0:T(8,128)(2,1)S(1)}, bf16[128,2048]{1,0:T(8,128)(2,1)S(1)}) fusion(bf16[2,128,2048]{2,1,0:T(8,128)(2,1)S(1)} %get-tuple-element.21, s32[]{:T(128)S(6)} %min.19, bf16[1,128,2048]{2,1,0:T(8,128)(2,1)} %constant_dynamic-slice_fusion, pred[]{:T(512)S(6)} %and.20, ...), kind=kOutput, calls=%fused_computation.74 | convolution fusion | flops 537657344 | bytes 7077893 | tf_op jit(solution)/shard_map/tr,dr->td/dot_general | solution.py:77
  232.3 1.4 collective-permute-start.3
  234.4 1.0 copy.135
  235.3 8.4 %collective-permute-done.3 = bf16[128,2048]{1,0:T(8,128)(2,1)S(1)} collective-permute-done((bf16[128,2048]{1,0:T(8,128)(2,1)S(1)}, bf16[128,2048]{1,0:T(8,128)(2,1)S(1)}, u32[]{:S(2)}, u32[]{:S(2)}) %collective-permute-start.3) | collective-permute-done | bytes 524320 | tf_op jit(solution)/shard_map/ppermute | solution.py:10
  244.2 0.9 fusion.74
  245.1 4.4 %fusion.71 = bf16[128,1024]{1,0:T(8,128)(2,1)} fusion(bf16[1,1024,2048]{2,1,0:T(8,128)(2,1)} %all-gather.6.cloned.1.call-done, bf16[128,2048]{1,0:T(8,128)(2,1)S(1)} %collective-permute-done.3, bf16[2,128,2048]{2,1,0:T(8,128)(2,1)S(1)} %copy-done.3, s32[]{:T(128)S(6)} %min.20, pred[]{:T(512)S(6)} %eq.14), kind=kOutput, calls=%fused_computation.37 | convolution fusion | flops 537264128 | bytes 5505029 | tf_op jit(solution)/shard_map/td,rd->tr/dot_general | solution.py:55
  250.2 1.0 reduce-scatter.17.cloned.1.call-done
  251.2 1.4 bitcast_convert_fusion
  252.5 22.0 %reduce-scatter.15.cloned.1.call-done = bf16[128,256]{1,0:T(8,128)(2,1)} async-done(((bf16[128,1024]{1,0:T(8,128)(2,1)}), bf16[128,256]{1,0:T(8,128)(2,1)}) %reduce-scatter.15.cloned.1.call-update) | async-done | bytes 65552 | tf_op jit(solution)/shard_map/reduce_scatter | solution.py:58
  274.5 14.2 %all_gather.31 = bf16[128,1024]{1,0:T(8,128)(2,1)S(1)} all-gather(bf16[128,256]{1,0:T(8,128)(2,1)} %reduce-scatter.15.cloned.1.call-done), channel_id=1, replica_groups=mesh['section'=4,'dp'=2,'tensor'=4] {'tensor'}, dimensions={1}, use_global_device_ids=true | all-gather | bytes 327680 | tf_op jit(solution)/shard_map/all_gather | solution.py:61
  288.7 4.7 %fusion.56 = bf16[1,2,128,2048]{3,2,1,0:T(8,128)(2,1)} fusion(bf16[1,2,128,2048]{3,2,1,0:T(8,128)(2,1)} %copy.135, s32[]{:T(128)S(6)} %min.20, bf16[128,1024]{1,0:T(8,128)(2,1)S(1)} %all_gather.31, bf16[1,2048,1024]{2,1,0:T(8,128)(2,1)} %all-gather.8.cloned.1.call-done, f32[16,8,16,128]{3,2,1,0:T(8,128)S(1)} %bitcast.276, ...), kind=kOutput, calls=%fused_computation.32 | convolution fusion | flops 537657344 | bytes 6553605 | tf_op jit(solution)/shard_map/tr,dr->td/dot_general | solution.py:77
  (89 shorter events, 10.9 us)
Async XLA Ops:
  7.2 18.8 %all-gather.6.cloned.1.call-start = ((), (), s32[]{:S(2)}) async-start(), calls=%async_computation.12 | async-start | bytes 6291456 | tf_op jit(solution)/shard_map/all_gather | solution.py:24
  7.9 23.4 %copy-start.3 = (bf16[2,128,2048]{2,1,0:T(8,128)(2,1)S(1)}, bf16[2,128,2048]{2,1,0:T(8,128)(2,1)}, u32[]{:S(2)}) copy-start(bf16[2,128,2048]{2,1,0:T(8,128)(2,1)} %param.7) | copy-start | bytes 3145732
  7.9 44.0 %reduce-scatter.7.cloned.1.call-start = ((), (), s32[]{:S(2)}) async-start(), calls=%async_computation.6 | async-start | bytes 327680 | tf_op jit(solution)/shard_map/reduce_scatter | solution.py:58
  8.0 24.1 %copy-start.13 = (s32[1,8]{1,0:T(1,128)S(1)}, s32[1,8]{1,0:T(1,128)}, u32[]{:S(2)}) copy-start(s32[1,8]{1,0:T(1,128)} %param.12) | copy-start | bytes 100
  8.0 24.8 %copy-start.14 = (s32[1,8]{1,0:T(1,128)S(1)}, s32[1,8]{1,0:T(1,128)}, u32[]{:S(2)}) copy-start(s32[1,8]{1,0:T(1,128)} %param.13) | copy-start | bytes 100
  8.0 25.6 %copy-start.4 = (bf16[1,2,128,2048]{3,2,1,0:T(8,128)(2,1)S(1)}, bf16[1,2,128,2048]{3,2,1,0:T(8,128)(2,1)}, u32[]{:S(2)}) copy-start(bf16[1,2,128,2048]{3,2,1,0:T(8,128)(2,1)} %param.8) | copy-start | bytes 3145732
  30.5 35.3 %all-gather.8.cloned.1.call-start = ((), (), s32[]{:S(2)}) async-start(), calls=%async_computation.13 | async-start | bytes 6291456 | tf_op jit(solution)/shard_map/all_gather | solution.py:25
  31.3 79.2 %reduce-scatter.9.cloned.1.call-start = ((), (), s32[]{:S(2)}) async-start(), calls=%async_computation.7 | async-start | bytes 327680 | tf_op jit(solution)/shard_map/reduce_scatter | solution.py:58
  31.3 4.8 %copy-start.12 = (bf16[1,1,128,128]{3,2,1,0:T(8,128)(2,1)S(1)}, bf16[1,1,128,128]{3,2,1,0:T(8,128)(2,1)}, u32[]{:S(2)}) copy-start(bf16[1,1,128,128]{3,2,1,0:T(8,128)(2,1)} %param.11) | copy-start | bytes 98308
  70.7 15.7 %collective-permute-start = (bf16[128,2048]{1,0:T(8,128)(2,1)}, bf16[128,2048]{1,0:T(8,128)(2,1)S(1)}, u32[]{:S(2)}, u32[]{:S(2)}) collective-permute-start(bf16[128,2048]{1,0:T(8,128)(2,1)} %get-tuple-element.18), channel_id=1, source_target_pairs={{8,0},{16,8},{24,16},{9,1},{17,9},{25,17},{10,2},{18,10},{26,18},{... | collective-permute-start | bytes 1572872 | tf_op jit(solution)/shard_map/ppermute | solution.py:10
  77.1 9.7 %copy-start = (bf16[1,1024,2048]{2,1,0:T(8,128)(2,1)S(1)}, bf16[1,1024,2048]{2,1,0:T(8,128)(2,1)}, u32[]{:S(2)}) copy-start(bf16[1,1024,2048]{2,1,0:T(8,128)(2,1)} %all-gather.6.cloned.1.call-done) | copy-start | bytes 12582916
  89.1 73.1 %reduce-scatter.11.cloned.1.call-start = ((), (), s32[]{:S(2)}) async-start(), calls=%async_computation.8 | async-start | bytes 327680 | tf_op jit(solution)/shard_map/reduce_scatter | solution.py:58
  110.4 20.3 %copy-start.5 = (bf16[16,8,16,128]{3,2,1,0:T(8,128)(2,1)S(1)}, bf16[16,8,16,128]{3,2,1,0:T(8,128)(2,1)}, u32[]{:S(2)}) copy-start(bf16[16,8,16,128]{3,2,1,0:T(8,128)(2,1)} %copy.73) | copy-start | bytes 1572868
  129.4 11.6 %collective-permute-start.1 = (bf16[128,2048]{1,0:T(8,128)(2,1)}, bf16[128,2048]{1,0:T(8,128)(2,1)S(1)}, u32[]{:S(2)}, u32[]{:S(2)}) collective-permute-start(bf16[128,2048]{1,0:T(8,128)(2,1)} %get-tuple-element.20), channel_id=1, source_target_pairs={{8,0},{16,8},{24,16},{9,1},{17,9},{25,17},{10,2},{18,10},{26,18},{... | collective-permute-start | bytes 1572872 | tf_op jit(solution)/shard_map/ppermute | solution.py:10
  132.8 8.7 %copy-start.1 = (bf16[1,1024,2048]{2,1,0:T(8,128)(2,1)S(1)}, bf16[1,1024,2048]{2,1,0:T(8,128)(2,1)}, u32[]{:S(2)}) copy-start(bf16[1,1024,2048]{2,1,0:T(8,128)(2,1)} %all-gather.6.cloned.1.call-done) | copy-start | bytes 12582916
  143.7 70.3 %reduce-scatter.13.cloned.1.call-start = ((), (), s32[]{:S(2)}) async-start(), calls=%async_computation.9 | async-start | bytes 327680 | tf_op jit(solution)/shard_map/reduce_scatter | solution.py:58
  144.4 38.3 %copy-start.9 = (bf16[128,2,128]{2,1,0:T(2,128)(2,1)S(1)}, bf16[128,2,128]{2,1,0:T(2,128)(2,1)}, u32[]{:S(2)}) copy-start(bf16[128,2,128]{2,1,0:T(2,128)(2,1)} %fusion.81) | copy-start | bytes 196612
  181.4 11.4 %collective-permute-start.2 = (bf16[128,2048]{1,0:T(8,128)(2,1)}, bf16[128,2048]{1,0:T(8,128)(2,1)S(1)}, u32[]{:S(2)}, u32[]{:S(2)}) collective-permute-start(bf16[128,2048]{1,0:T(8,128)(2,1)} %get-tuple-element.22), channel_id=1, source_target_pairs={{8,0},{16,8},{24,16},{9,1},{17,9},{25,17},{10,2},{18,10},{26,18},{... | collective-permute-start | bytes 1572872 | tf_op jit(solution)/shard_map/ppermute | solution.py:10
  184.7 8.5 %copy-start.2 = (bf16[1,1024,2048]{2,1,0:T(8,128)(2,1)S(1)}, bf16[1,1024,2048]{2,1,0:T(8,128)(2,1)}, u32[]{:S(2)}) copy-start(bf16[1,1024,2048]{2,1,0:T(8,128)(2,1)} %all-gather.6.cloned.1.call-done) | copy-start | bytes 12582916
  195.5 55.6 %reduce-scatter.17.cloned.1.call-start = ((), (), s32[]{:S(2)}) async-start(), calls=%async_computation.11 | async-start | bytes 98304 | tf_op jit(solution)/shard_map/reduce_scatter | solution.py:101
  195.8 37.9 %copy-start.6 = (f32[2,128,128]{2,1,0:T(8,128)S(1)}, f32[2,128,128]{2,1,0:T(8,128)}, u32[]{:S(2)}) copy-start(f32[2,128,128]{2,1,0:T(8,128)} %fusion.116) | copy-start | bytes 393220
  214.0 19.7 %copy-start.8 = (bf16[128,2,128]{2,1,0:T(2,128)(2,1)S(1)}, bf16[128,2,128]{2,1,0:T(2,128)(2,1)}, u32[]{:S(2)}) copy-start(bf16[128,2,128]{2,1,0:T(2,128)(2,1)} %fusion.83) | copy-start | bytes 196612
  214.0 19.9 %copy-start.10 = (bf16[128,2,128]{2,1,0:T(2,128)(2,1)S(1)}, bf16[128,2,128]{2,1,0:T(2,128)(2,1)}, u32[]{:S(2)}) copy-start(bf16[128,2,128]{2,1,0:T(2,128)(2,1)} %fusion.85) | copy-start | bytes 196612
  214.0 20.1 %copy-start.11 = (bf16[128,2,128]{2,1,0:T(2,128)(2,1)S(1)}, bf16[128,2,128]{2,1,0:T(2,128)(2,1)}, u32[]{:S(2)}) copy-start(bf16[128,2,128]{2,1,0:T(2,128)(2,1)} %fusion.87) | copy-start | bytes 196612
  232.2 12.0 %copy-start.7 = (bf16[128,2,128]{2,1,0:T(2,128)(2,1)S(1)}, bf16[128,2,128]{2,1,0:T(2,128)(2,1)}, u32[]{:S(2)}) copy-start(bf16[128,2,128]{2,1,0:T(2,128)(2,1)} %fusion.89) | copy-start | bytes 196612
  232.3 11.5 %collective-permute-start.3 = (bf16[128,2048]{1,0:T(8,128)(2,1)S(1)}, bf16[128,2048]{1,0:T(8,128)(2,1)S(1)}, u32[]{:S(2)}, u32[]{:S(2)}) collective-permute-start(bf16[128,2048]{1,0:T(8,128)(2,1)S(1)} %get-tuple-element.24), channel_id=1, source_target_pairs={{8,0},{16,8},{24,16},{9,1},{17,9},{25,17},{10,2},{18,10},{26,18},{... | collective-permute-start | bytes 1572872 | tf_op jit(solution)/shard_map/ppermute | solution.py:10
  245.1 29.4 %reduce-scatter.15.cloned.1.call-start = ((), (), s32[]{:S(2)}) async-start(), calls=%async_computation.10 | async-start | bytes 327680 | tf_op jit(solution)/shard_map/reduce_scatter | solution.py:58
Sparse Core Ops, SparseCore 0:
  9.5 16.3 all-gather.5
  30.7 21.1 reduce-scatter.6
  53.4 11.8 all-gather.7
  89.2 21.1 reduce-scatter.8
  143.8 18.3 reduce-scatter.10
  195.6 18.3 reduce-scatter.12
  245.2 5.9 reduce-scatter.16
  253.4 21.0 reduce-scatter.14
where the time goes:
time: 301 us; the launch traced here: 300 us
  waiting for transfers between devices  140 us (47%)
  blocking collectives  72.7 us (24%)
  matrix products  51 us (17%)
  between operations  14.6 us (5%)
  local copies, waits for them, and re-layouts  12.8 us (4%)
  starting transfers between devices  5.59 us (2%)
  other arithmetic  3.35 us (1%)
    reduce_scatter x5, waiting for transfers between devices, on_device(): lax.psum_scatter(partial_value.astype(jnp.bfloat16), 'tensor', scatter_di...  91.2 us
    all_gather x5, blocking collectives, on_device(): rank_act = lax.all_gather(share, 'tensor', axis=1, tiled=True)  70.8 us
    ppermute x4, waiting for transfers between devices, shifted(): lax.ppermute(value, axis, [(source, source + steps) for source in range(i...  28.5 us
    dot_general x5, matrix products, on_device(): jnp.einsum('tr,dr->td', rank_act, right_full, preferred_element_type=jnp....  23.1 us
    all_gather x1, waiting for transfers between devices, on_device(): lax.all_gather(factor_a[0], 'dp', axis=0, tiled=True)  17.9 us
    dot_general x5, matrix products, on_device(): jnp.einsum('td,rd->tr', cot_now, left_full, preferred_element_type=jnp.fl...  15.7 us
    unnamed x43, local copies, waits for them, and re-layouts  9.95 us
  transfers between devices with their start and end apart: 12, of which 11 were waited for; matrix products, arithmetic and copies ran while one was open for 10% of the time, Pallas kernels for 0%

commit v1 on v0

--- a/solution.py
+++ b/solution.py
@@ -58,7 +58,6 @@
         share = lax.psum_scatter(
             partial_value.astype(jnp.bfloat16), "tensor", scatter_dimension=1, tiled=True
         )
-        rank_act = lax.all_gather(share, "tensor", axis=1, tiled=True)
         picked_cot = jnp.einsum(
             "tlc,nl->tnc",
             cot_now.reshape(tokens_here, local_blocks, block_size),
@@ -74,9 +73,38 @@
         sparse_grad = jnp.einsum(
             "tnr,nl->tlr", both_parts, row_double, preferred_element_type=jnp.float32
         )
-        dense_grad = jnp.einsum(
-            "tr,dr->td", rank_act, right_full, preferred_element_type=jnp.float32
+        size, index, width = (lax.axis_size("tensor"), lax.axis_index("tensor"), share.shape[1])
+        forward = [(i, (i + 1) % size) for i in range(size)]
+        backward = [(i, (i - 1) % size) for i in range(size)]
+        half = size // 2
+        from_left = from_right = share
+        subtotal = jnp.einsum(
+            "tr,dr->td",
+            share,
+            lax.dynamic_slice_in_dim(right_full, index * width, share.shape[1], axis=1),
+            preferred_element_type=jnp.float32,
         )
+        for turn in range(1, half + 1):
+            from_left = lax.ppermute(from_left, "tensor", forward)
+            if turn < size - half:
+                from_right = lax.ppermute(from_right, "tensor", backward)
+                subtotal = subtotal + jnp.einsum(
+                    "tr,dr->td",
+                    from_right,
+                    lax.dynamic_slice_in_dim(
+                        right_full, (index + turn) % size * width, from_right.shape[1], axis=1
+                    ),
+                    preferred_element_type=jnp.float32,
+                )
+            subtotal = subtotal + jnp.einsum(
+                "tr,dr->td",
+                from_left,
+                lax.dynamic_slice_in_dim(
+                    right_full, (index - turn) % size * width, from_left.shape[1], axis=1
+                ),
+                preferred_element_type=jnp.float32,
+            )
+        dense_grad = subtotal
         grad_out = (dense_grad + sparse_grad.reshape(tokens_here, local_width)).astype(jnp.bfloat16)
         current = lax.dynamic_index_in_dim(grads_in, slot_pos, 0, keepdims=False)
         grads_in = lax.dynamic_update_index_in_dim(

time: 301 us -> 285 us (0.947)
  blocking collectives: 72.7 us -> 1.85 us
  waiting for transfers between devices: 140 us -> 181 us
  starting transfers between devices: 5.59 us -> 17.5 us
    all_gather x5 -> x0, blocking collectives: 70.8 us -> none  [on_device(): rank_act = lax.all_gather(share, 'tensor', axis=1, tiled=True)]
    ppermute x0 -> x15, waiting for transfers between devices: none -> 29.2 us  [the longest x10 29.2 us: on_device(): from_left = lax.ppermute(from_left, 'tensor', forward)]
    ppermute x0 -> x15, starting transfers between devices: none -> 11.9 us  [the longest x10 9.79 us: on_device(): from_left = lax.ppermute(from_left, 'tensor', forward)]
    all_gather x1, waiting for transfers between devices: 0.01 us -> 11.4 us  [on_device(): lax.all_gather(factor_b[0], 'dp', axis=0, tiled=True)]
    dot_general x5 -> x20, matrix products: 23.1 us -> 25.9 us  [the longest x5 8.82 us: on_device(): jnp.einsum('tr,dr->td', share, lax.dynamic_slice_in_dim(right_full, index...]
    unnamed x43 -> x63, local copies, waits for them, and re-layouts: 9.95 us -> 10.8 us
  transfers between devices with their start and end apart: 12 -> 27, of which waited for: 11 -> 21; matrix products, arithmetic and copies ran while one was open for 10% -> 17% of each run, Pallas kernels for 0% -> 0%
where the time goes in v1:
time: 285 us; the launch traced here: 284 us
  waiting for transfers between devices  181 us (64%)
  matrix products  52.1 us (18%)
  starting transfers between devices  17.5 us (6%)
  between operations  14.9 us (5%)
  local copies, waits for them, and re-layouts  13.7 us (5%)
  other arithmetic  3.35 us (1%)
    reduce_scatter x5, waiting for transfers between devices, on_device(): lax.psum_scatter(partial_value.astype(jnp.bfloat16), 'tensor', scatter_di...  89.6 us
    ppermute x4, waiting for transfers between devices, shifted(): lax.ppermute(value, axis, [(source, source + steps) for source in range(i...  30.3 us
    ppermute x10, waiting for transfers between devices, on_device(): from_left = lax.ppermute(from_left, 'tensor', forward)  29.2 us
    all_gather x1, waiting for transfers between devices, on_device(): lax.all_gather(factor_a[0], 'dp', axis=0, tiled=True)  17.9 us
    dot_general x5, matrix products, on_device(): jnp.einsum('td,rd->tr', cot_now, left_full, preferred_element_type=jnp.fl...  15.7 us
    all_gather x1, waiting for transfers between devices, on_device(): lax.all_gather(factor_b[0], 'dp', axis=0, tiled=True)  11.4 us
    unnamed x63, local copies, waits for them, and re-layouts  10.8 us
    ppermute x10, starting transfers between devices, on_device(): from_left = lax.ppermute(from_left, 'tensor', forward)  9.79 us
  transfers between devices with their start and end apart: 27, of which 21 were waited for; matrix products, arithmetic and copies ran while one was open for 17% of the time, Pallas kernels for 0%

profile of v1, /device:TPU:0, one launch (start us, length us, event | category | flops | bytes accessed | tf_op | source)
XLA Modules:
  0.0 284.5 jit_solution(15317015601307418098)
XLA Ops:
  8.0 17.9 %all-gather.6.cloned.1.call-done = bf16[1,1024,2048]{2,1,0:T(8,128)(2,1)} async-done(((bf16[1,512,2048]{2,1,0:T(8,128)(2,1)}), bf16[1,1024,2048]{2,1,0:T(8,128)(2,1)}) %all-gather.6.cloned.1.call-update) | async-done | bytes 4194320 | tf_op jit(solution)/shard_map/all_gather | solution.py:24
  25.9 4.6 %fusion.23 = bf16[128,1024]{1,0:T(8,128)(2,1)} fusion(bf16[1,1024,2048]{2,1,0:T(8,128)(2,1)} %all-gather.6.cloned.1.call-done, bf16[2,128,2048]{2,1,0:T(8,128)(2,1)} %param.7, s32[]{:T(128)S(6)} %min.16, pred[]{:T(512)S(6)} %eq.49), kind=kOutput, calls=%fused_computation.38 | convolution fusion | flops 537264128 | bytes 4980741 | tf_op jit(solution)/shard_map/td,rd->tr/dot_general | solution.py:55
  33.6 1.4 dynamic-slice_bitcast_fusion
  36.2 1.9 all-gather.2
  39.0 12.9 %reduce-scatter.7.cloned.1.call-done = bf16[128,256]{1,0:T(8,128)(2,1)} async-done(((bf16[128,1024]{1,0:T(8,128)(2,1)}), bf16[128,256]{1,0:T(8,128)(2,1)}) %reduce-scatter.7.cloned.1.call-update) | async-done | bytes 65552 | tf_op jit(solution)/shard_map/reduce_scatter | solution.py:58
  52.3 1.6 collective-permute-start.1
  53.9 11.4 %all-gather.8.cloned.1.call-done = bf16[1,2048,1024]{2,1,0:T(8,128)(2,1)} async-done(((bf16[1,1024,1024]{2,1,0:T(8,128)(2,1)}), bf16[1,2048,1024]{2,1,0:T(8,128)(2,1)}) %all-gather.8.cloned.1.call-update) | async-done | bytes 4194320 | tf_op jit(solution)/shard_map/all_gather | solution.py:25
  65.3 1.9 fusion.77
  67.2 1.8 collective-permute-start.2
  69.0 1.7 convolution_add_fusion.14
  71.3 2.2 collective-permute-done.2
  73.6 1.5 bitcast_dynamic-update-slice_fusion.3
  78.5 2.0 copy.73
  82.2 8.3 %collective-permute-done.3 = bf16[128,2048]{1,0:T(8,128)(2,1)S(1)} collective-permute-done((bf16[128,2048]{1,0:T(8,128)(2,1)}, bf16[128,2048]{1,0:T(8,128)(2,1)S(1)}, u32[]{:S(2)}, u32[]{:S(2)}) %collective-permute-start.3) | collective-permute-done | bytes 524320 | tf_op jit(solution)/shard_map/ppermute | solution.py:10
  91.0 2.2 fusion.26
  93.9 18.8 %reduce-scatter.9.cloned.1.call-done = bf16[128,256]{1,0:T(8,128)(2,1)} async-done(((bf16[128,1024]{1,0:T(8,128)(2,1)}), bf16[128,256]{1,0:T(8,128)(2,1)}) %reduce-scatter.9.cloned.1.call-update) | async-done | bytes 65552 | tf_op jit(solution)/shard_map/reduce_scatter | solution.py:58
  113.1 1.5 collective-permute-start.5
  114.7 1.7 fusion.75
  116.4 3.0 %collective-permute-done.5 = bf16[128,256]{1,0:T(8,128)(2,1)S(1)} collective-permute-done((bf16[128,256]{1,0:T(8,128)(2,1)}, bf16[128,256]{1,0:T(8,128)(2,1)S(1)}, u32[]{:S(2)}, u32[]{:S(2)}) %collective-permute-start.5) | collective-permute-done | bytes 65568 | tf_op jit(solution)/shard_map/ppermute | solution.py:88
  119.4 1.7 convolution_add_fusion.11
  121.6 3.8 %collective-permute-done.6 = bf16[128,256]{1,0:T(8,128)(2,1)S(1)} collective-permute-done((bf16[128,256]{1,0:T(8,128)(2,1)S(1)}, bf16[128,256]{1,0:T(8,128)(2,1)S(1)}, u32[]{:S(2)}, u32[]{:S(2)}) %collective-permute-start.6) | collective-permute-done | bytes 65568 | tf_op jit(solution)/shard_map/ppermute | solution.py:88
  125.5 1.5 bitcast_dynamic-update-slice_fusion.2
  132.2 6.4 %collective-permute-done.7 = bf16[128,2048]{1,0:T(8,128)(2,1)S(1)} collective-permute-done((bf16[128,2048]{1,0:T(8,128)(2,1)}, bf16[128,2048]{1,0:T(8,128)(2,1)S(1)}, u32[]{:S(2)}, u32[]{:S(2)}) %collective-permute-start.7) | collective-permute-done | bytes 524320 | tf_op jit(solution)/shard_map/ppermute | solution.py:10
  139.1 2.2 fusion.29
  142.0 17.9 %reduce-scatter.11.cloned.1.call-done = bf16[128,256]{1,0:T(8,128)(2,1)} async-done(((bf16[128,1024]{1,0:T(8,128)(2,1)}), bf16[128,256]{1,0:T(8,128)(2,1)}) %reduce-scatter.11.cloned.1.call-update) | async-done | bytes 65552 | tf_op jit(solution)/shard_map/reduce_scatter | solution.py:58
  160.4 1.6 collective-permute-start.9
  161.9 1.7 fusion.73
  163.7 3.0 %collective-permute-done.9 = bf16[128,256]{1,0:T(8,128)(2,1)S(1)} collective-permute-done((bf16[128,256]{1,0:T(8,128)(2,1)}, bf16[128,256]{1,0:T(8,128)(2,1)S(1)}, u32[]{:S(2)}, u32[]{:S(2)}) %collective-permute-start.9) | collective-permute-done | bytes 65568 | tf_op jit(solution)/shard_map/ppermute | solution.py:88
  166.7 1.7 convolution_add_fusion.8
  168.9 3.8 %collective-permute-done.10 = bf16[128,256]{1,0:T(8,128)(2,1)S(1)} collective-permute-done((bf16[128,256]{1,0:T(8,128)(2,1)S(1)}, bf16[128,256]{1,0:T(8,128)(2,1)S(1)}, u32[]{:S(2)}, u32[]{:S(2)}) %collective-permute-start.10) | collective-permute-done | bytes 65568 | tf_op jit(solution)/shard_map/ppermute | solution.py:88
  172.7 1.5 bitcast_dynamic-update-slice_fusion.1
  178.7 7.1 %collective-permute-done.11 = bf16[128,2048]{1,0:T(8,128)(2,1)S(1)} collective-permute-done((bf16[128,2048]{1,0:T(8,128)(2,1)}, bf16[128,2048]{1,0:T(8,128)(2,1)S(1)}, u32[]{:S(2)}, u32[]{:S(2)}) %collective-permute-start.11) | collective-permute-done | bytes 524320 | tf_op jit(solution)/shard_map/ppermute | solution.py:10
  186.3 2.2 fusion.32
  189.2 18.0 %reduce-scatter.13.cloned.1.call-done = bf16[128,256]{1,0:T(8,128)(2,1)} async-done(((bf16[128,1024]{1,0:T(8,128)(2,1)}), bf16[128,256]{1,0:T(8,128)(2,1)}) %reduce-scatter.13.cloned.1.call-update) | async-done | bytes 65552 | tf_op jit(solution)/shard_map/reduce_scatter | solution.py:58
  207.6 1.6 collective-permute-start.13
  209.2 1.7 fusion.71
  211.0 2.9 %collective-permute-done.13 = bf16[128,256]{1,0:T(8,128)(2,1)S(1)} collective-permute-done((bf16[128,256]{1,0:T(8,128)(2,1)}, bf16[128,256]{1,0:T(8,128)(2,1)S(1)}, u32[]{:S(2)}, u32[]{:S(2)}) %collective-permute-start.13) | collective-permute-done | bytes 65568 | tf_op jit(solution)/shard_map/ppermute | solution.py:88
  213.9 1.7 convolution_add_fusion.5
  216.2 3.8 %collective-permute-done.14 = bf16[128,256]{1,0:T(8,128)(2,1)S(1)} collective-permute-done((bf16[128,256]{1,0:T(8,128)(2,1)S(1)}, bf16[128,256]{1,0:T(8,128)(2,1)S(1)}, u32[]{:S(2)}, u32[]{:S(2)}) %collective-permute-start.14) | collective-permute-done | bytes 65568 | tf_op jit(solution)/shard_map/ppermute | solution.py:88
  220.7 1.4 collective-permute-start.15
  223.8 8.5 %collective-permute-done.15 = bf16[128,2048]{1,0:T(8,128)(2,1)S(1)} collective-permute-done((bf16[128,2048]{1,0:T(8,128)(2,1)S(1)}, bf16[128,2048]{1,0:T(8,128)(2,1)S(1)}, u32[]{:S(2)}, u32[]{:S(2)}) %collective-permute-start.15) | collective-permute-done | bytes 524320 | tf_op jit(solution)/shard_map/ppermute | solution.py:10
  233.7 4.4 %fusion.35 = bf16[128,1024]{1,0:T(8,128)(2,1)} fusion(bf16[1,1024,2048]{2,1,0:T(8,128)(2,1)} %all-gather.6.cloned.1.call-done, bf16[128,2048]{1,0:T(8,128)(2,1)S(1)} %collective-permute-done.15, bf16[2,128,2048]{2,1,0:T(8,128)(2,1)S(1)} %copy-done.8, s32[]{:T(128)S(6)} %min.20, pred[]{:T(512)S(6)} %eq.49), kind=kOutput, calls=%fused_computation.42 | convolution fusion | flops 537264128 | bytes 5505029 | tf_op jit(solution)/shard_map/td,rd->tr/dot_general | solution.py:55
  241.2 22.0 %reduce-scatter.15.cloned.1.call-done = bf16[128,256]{1,0:T(8,128)(2,1)} async-done(((bf16[128,1024]{1,0:T(8,128)(2,1)}), bf16[128,256]{1,0:T(8,128)(2,1)}) %reduce-scatter.15.cloned.1.call-update) | async-done | bytes 65552 | tf_op jit(solution)/shard_map/reduce_scatter | solution.py:58
  263.6 1.6 collective-permute-start.17
  265.2 1.7 fusion.69
  267.0 2.9 %collective-permute-done.17 = bf16[128,256]{1,0:T(8,128)(2,1)S(1)} collective-permute-done((bf16[128,256]{1,0:T(8,128)(2,1)}, bf16[128,256]{1,0:T(8,128)(2,1)S(1)}, u32[]{:S(2)}, u32[]{:S(2)}) %collective-permute-start.17) | collective-permute-done | bytes 65568 | tf_op jit(solution)/shard_map/ppermute | solution.py:88
  269.9 1.7 convolution_add_fusion.2
  272.1 3.8 %collective-permute-done.18 = bf16[128,256]{1,0:T(8,128)(2,1)S(1)} collective-permute-done((bf16[128,256]{1,0:T(8,128)(2,1)S(1)}, bf16[128,256]{1,0:T(8,128)(2,1)S(1)}, u32[]{:S(2)}, u32[]{:S(2)}) %collective-permute-start.18) | collective-permute-done | bytes 65568 | tf_op jit(solution)/shard_map/ppermute | solution.py:88
  (149 shorter events, 37.0 us)
Async XLA Ops:
  7.2 18.8 %all-gather.6.cloned.1.call-start = ((), (), s32[]{:S(2)}) async-start(), calls=%async_computation.12 | async-start | bytes 6291456 | tf_op jit(solution)/shard_map/all_gather | solution.py:24
  7.9 23.5 %copy-start.8 = (bf16[2,128,2048]{2,1,0:T(8,128)(2,1)S(1)}, bf16[2,128,2048]{2,1,0:T(8,128)(2,1)}, u32[]{:S(2)}) copy-start(bf16[2,128,2048]{2,1,0:T(8,128)(2,1)} %param.7) | copy-start | bytes 3145732
  7.9 44.0 %reduce-scatter.7.cloned.1.call-start = ((), (), s32[]{:S(2)}) async-start(), calls=%async_computation.6 | async-start | bytes 327680 | tf_op jit(solution)/shard_map/reduce_scatter | solution.py:58
  8.0 24.1 %copy-start.23 = (s32[1,8]{1,0:T(1,128)S(1)}, s32[1,8]{1,0:T(1,128)}, u32[]{:S(2)}) copy-start(s32[1,8]{1,0:T(1,128)} %param.12) | copy-start | bytes 100
  8.0 24.9 %copy-start.24 = (s32[1,8]{1,0:T(1,128)S(1)}, s32[1,8]{1,0:T(1,128)}, u32[]{:S(2)}) copy-start(s32[1,8]{1,0:T(1,128)} %param.13) | copy-start | bytes 100
  8.0 25.6 %copy-start.9 = (bf16[1,2,128,2048]{3,2,1,0:T(8,128)(2,1)S(1)}, bf16[1,2,128,2048]{3,2,1,0:T(8,128)(2,1)}, u32[]{:S(2)}) copy-start(bf16[1,2,128,2048]{3,2,1,0:T(8,128)(2,1)} %param.8) | copy-start | bytes 3145732
  30.5 34.8 %all-gather.8.cloned.1.call-start = ((), (), s32[]{:S(2)}) async-start(), calls=%async_computation.13 | async-start | bytes 6291456 | tf_op jit(solution)/shard_map/all_gather | solution.py:25
  31.3 81.4 %reduce-scatter.9.cloned.1.call-start = ((), (), s32[]{:S(2)}) async-start(), calls=%async_computation.7 | async-start | bytes 327680 | tf_op jit(solution)/shard_map/reduce_scatter | solution.py:58
  51.9 17.2 %collective-permute-start = (bf16[128,256]{1,0:T(8,128)(2,1)}, bf16[128,256]{1,0:T(8,128)(2,1)S(1)}, u32[]{:S(2)}, u32[]{:S(2)}) collective-permute-start(bf16[128,256]{1,0:T(8,128)(2,1)} %reduce-scatter.7.cloned.1.call-done), channel_id=1, source_target_pairs={{0,3},{1,0},{2,1},{3,2},{4,7},{5,4},{6,5},{7,6},{8,11},{9,8},{10,9... | collective-permute-start | bytes 196616 | tf_op jit(solution)/shard_map/ppermute | solution.py:90
  52.3 14.9 %collective-permute-start.1 = (bf16[128,256]{1,0:T(8,128)(2,1)}, bf16[128,256]{1,0:T(8,128)(2,1)S(1)}, u32[]{:S(2)}, u32[]{:S(2)}) collective-permute-start(bf16[128,256]{1,0:T(8,128)(2,1)} %reduce-scatter.7.cloned.1.call-done), channel_id=1, source_target_pairs={{0,1},{1,2},{2,3},{3,0},{4,5},{5,6},{6,7},{7,4},{8,9},{9,10},{10,1... | collective-permute-start | bytes 196616 | tf_op jit(solution)/shard_map/ppermute | solution.py:88
  67.2 6.2 %collective-permute-start.2 = (bf16[128,256]{1,0:T(8,128)(2,1)S(1)}, bf16[128,256]{1,0:T(8,128)(2,1)S(1)}, u32[]{:S(2)}, u32[]{:S(2)}) collective-permute-start(bf16[128,256]{1,0:T(8,128)(2,1)S(1)} %collective-permute-done.1), channel_id=1, source_target_pairs={{0,1},{1,2},{2,3},{3,0},{4,5},{5,6},{6,7},{7,4},{8,9},{9,10},{10,1... | collective-permute-start | bytes 196616 | tf_op jit(solution)/shard_map/ppermute | solution.py:88
  75.1 15.4 %collective-permute-start.3 = (bf16[128,2048]{1,0:T(8,128)(2,1)}, bf16[128,2048]{1,0:T(8,128)(2,1)S(1)}, u32[]{:S(2)}, u32[]{:S(2)}) collective-permute-start(bf16[128,2048]{1,0:T(8,128)(2,1)} %get-tuple-element.18), channel_id=1, source_target_pairs={{8,0},{16,8},{24,16},{9,1},{17,9},{25,17},{10,2},{18,10},{26,18},{... | collective-permute-start | bytes 1572872 | tf_op jit(solution)/shard_map/ppermute | solution.py:10
  80.4 10.5 %copy-start.5 = (bf16[1,1024,2048]{2,1,0:T(8,128)(2,1)S(1)}, bf16[1,1024,2048]{2,1,0:T(8,128)(2,1)}, u32[]{:S(2)}) copy-start(bf16[1,1024,2048]{2,1,0:T(8,128)(2,1)} %all-gather.6.cloned.1.call-done) | copy-start | bytes 12582916
  93.2 66.7 %reduce-scatter.11.cloned.1.call-start = ((), (), s32[]{:S(2)}) async-start(), calls=%async_computation.8 | async-start | bytes 327680 | tf_op jit(solution)/shard_map/reduce_scatter | solution.py:58
  112.7 8.5 %copy-start.1 = (bf16[1,2048,1024]{2,1,0:T(8,128)(2,1)S(1)}, bf16[1,2048,1024]{2,1,0:T(8,128)(2,1)}, u32[]{:S(2)}) copy-start(bf16[1,2048,1024]{2,1,0:T(8,128)(2,1)} %all-gather.8.cloned.1.call-done) | copy-start | bytes 12582916
  112.7 12.8 %copy-start.12 = (bf16[1,128,2048]{2,1,0:T(8,128)(2,1)S(1)}, bf16[1,128,2048]{2,1,0:T(8,128)(2,1)}, u32[]{:S(2)}) copy-start(bf16[1,128,2048]{2,1,0:T(8,128)(2,1)} %constant_dynamic-slice_fusion.2) | copy-start | bytes 1572868
  112.7 6.8 %collective-permute-start.4 = (bf16[128,256]{1,0:T(8,128)(2,1)}, bf16[128,256]{1,0:T(8,128)(2,1)S(1)}, u32[]{:S(2)}, u32[]{:S(2)}) collective-permute-start(bf16[128,256]{1,0:T(8,128)(2,1)} %reduce-scatter.9.cloned.1.call-done), channel_id=1, source_target_pairs={{0,3},{1,0},{2,1},{3,2},{4,7},{5,4},{6,5},{7,6},{8,11},{9,8},{10,9... | collective-permute-start | bytes 196616 | tf_op jit(solution)/shard_map/ppermute | solution.py:90
  113.1 6.3 %collective-permute-start.5 = (bf16[128,256]{1,0:T(8,128)(2,1)}, bf16[128,256]{1,0:T(8,128)(2,1)S(1)}, u32[]{:S(2)}, u32[]{:S(2)}) collective-permute-start(bf16[128,256]{1,0:T(8,128)(2,1)} %reduce-scatter.9.cloned.1.call-done), channel_id=1, source_target_pairs={{0,1},{1,2},{2,3},{3,0},{4,5},{5,6},{6,7},{7,4},{8,9},{9,10},{10,1... | collective-permute-start | bytes 196616 | tf_op jit(solution)/shard_map/ppermute | solution.py:88
  119.4 6.1 %collective-permute-start.6 = (bf16[128,256]{1,0:T(8,128)(2,1)S(1)}, bf16[128,256]{1,0:T(8,128)(2,1)S(1)}, u32[]{:S(2)}, u32[]{:S(2)}) collective-permute-start(bf16[128,256]{1,0:T(8,128)(2,1)S(1)} %collective-permute-done.5), channel_id=1, source_target_pairs={{0,1},{1,2},{2,3},{3,0},{4,5},{5,6},{6,7},{7,4},{8,9},{9,10},{10,1... | collective-permute-start | bytes 196616 | tf_op jit(solution)/shard_map/ppermute | solution.py:88
  121.1 7.2 %copy-start.11 = (bf16[16,8,16,128]{3,2,1,0:T(8,128)(2,1)S(1)}, bf16[16,8,16,128]{3,2,1,0:T(8,128)(2,1)}, u32[]{:S(2)}) copy-start(bf16[16,8,16,128]{3,2,1,0:T(8,128)(2,1)} %copy.73) | copy-start | bytes 1572868
  127.0 11.6 %collective-permute-start.7 = (bf16[128,2048]{1,0:T(8,128)(2,1)}, bf16[128,2048]{1,0:T(8,128)(2,1)S(1)}, u32[]{:S(2)}, u32[]{:S(2)}) collective-permute-start(bf16[128,2048]{1,0:T(8,128)(2,1)} %get-tuple-element.20), channel_id=1, source_target_pairs={{8,0},{16,8},{24,16},{9,1},{17,9},{25,17},{10,2},{18,10},{26,18},{... | collective-permute-start | bytes 1572872 | tf_op jit(solution)/shard_map/ppermute | solution.py:10
  130.4 8.7 %copy-start.6 = (bf16[1,1024,2048]{2,1,0:T(8,128)(2,1)S(1)}, bf16[1,1024,2048]{2,1,0:T(8,128)(2,1)}, u32[]{:S(2)}) copy-start(bf16[1,1024,2048]{2,1,0:T(8,128)(2,1)} %all-gather.6.cloned.1.call-done) | copy-start | bytes 12582916
  141.3 65.9 %reduce-scatter.13.cloned.1.call-start = ((), (), s32[]{:S(2)}) async-start(), calls=%async_computation.9 | async-start | bytes 327680 | tf_op jit(solution)/shard_map/reduce_scatter | solution.py:58
  159.9 8.5 %copy-start.2 = (bf16[1,2048,1024]{2,1,0:T(8,128)(2,1)S(1)}, bf16[1,2048,1024]{2,1,0:T(8,128)(2,1)}, u32[]{:S(2)}) copy-start(bf16[1,2048,1024]{2,1,0:T(8,128)(2,1)} %all-gather.8.cloned.1.call-done) | copy-start | bytes 12582916
  159.9 12.8 %copy-start.13 = (bf16[1,128,2048]{2,1,0:T(8,128)(2,1)S(1)}, bf16[1,128,2048]{2,1,0:T(8,128)(2,1)}, u32[]{:S(2)}) copy-start(bf16[1,128,2048]{2,1,0:T(8,128)(2,1)} %constant_dynamic-slice_fusion.1) | copy-start | bytes 1572868
  159.9 6.8 %collective-permute-start.8 = (bf16[128,256]{1,0:T(8,128)(2,1)}, bf16[128,256]{1,0:T(8,128)(2,1)S(1)}, u32[]{:S(2)}, u32[]{:S(2)}) collective-permute-start(bf16[128,256]{1,0:T(8,128)(2,1)} %reduce-scatter.11.cloned.1.call-done), channel_id=1, source_target_pairs={{0,3},{1,0},{2,1},{3,2},{4,7},{5,4},{6,5},{7,6},{8,11},{9,8},{10,9... | collective-permute-start | bytes 196616 | tf_op jit(solution)/shard_map/ppermute | solution.py:90
  160.4 6.3 %collective-permute-start.9 = (bf16[128,256]{1,0:T(8,128)(2,1)}, bf16[128,256]{1,0:T(8,128)(2,1)S(1)}, u32[]{:S(2)}, u32[]{:S(2)}) collective-permute-start(bf16[128,256]{1,0:T(8,128)(2,1)} %reduce-scatter.11.cloned.1.call-done), channel_id=1, source_target_pairs={{0,1},{1,2},{2,3},{3,0},{4,5},{5,6},{6,7},{7,4},{8,9},{9,10},{10,1... | collective-permute-start | bytes 196616 | tf_op jit(solution)/shard_map/ppermute | solution.py:88
  166.7 6.1 %collective-permute-start.10 = (bf16[128,256]{1,0:T(8,128)(2,1)S(1)}, bf16[128,256]{1,0:T(8,128)(2,1)S(1)}, u32[]{:S(2)}, u32[]{:S(2)}) collective-permute-start(bf16[128,256]{1,0:T(8,128)(2,1)S(1)} %collective-permute-done.9), channel_id=1, source_target_pairs={{0,1},{1,2},{2,3},{3,0},{4,5},{5,6},{6,7},{7,4},{8,9},{9,10},{10,1... | collective-permute-start | bytes 196616 | tf_op jit(solution)/shard_map/ppermute | solution.py:88
  168.4 7.2 %copy-start.19 = (bf16[128,2,128]{2,1,0:T(2,128)(2,1)S(1)}, bf16[128,2,128]{2,1,0:T(2,128)(2,1)}, u32[]{:S(2)}) copy-start(bf16[128,2,128]{2,1,0:T(2,128)(2,1)} %fusion.45) | copy-start | bytes 196612
  174.3 11.6 %collective-permute-start.11 = (bf16[128,2048]{1,0:T(8,128)(2,1)}, bf16[128,2048]{1,0:T(8,128)(2,1)S(1)}, u32[]{:S(2)}, u32[]{:S(2)}) collective-permute-start(bf16[128,2048]{1,0:T(8,128)(2,1)} %get-tuple-element.22), channel_id=1, source_target_pairs={{8,0},{16,8},{24,16},{9,1},{17,9},{25,17},{10,2},{18,10},{26,18},{... | collective-permute-start | bytes 1572872 | tf_op jit(solution)/shard_map/ppermute | solution.py:10
  176.9 9.4 %copy-start.7 = (bf16[1,1024,2048]{2,1,0:T(8,128)(2,1)S(1)}, bf16[1,1024,2048]{2,1,0:T(8,128)(2,1)}, u32[]{:S(2)}) copy-start(bf16[1,1024,2048]{2,1,0:T(8,128)(2,1)} %all-gather.6.cloned.1.call-done) | copy-start | bytes 12582916
  188.6 51.2 %reduce-scatter.17.cloned.1.call-start = ((), (), s32[]{:S(2)}) async-start(), calls=%async_computation.11 | async-start | bytes 98304 | tf_op jit(solution)/shard_map/reduce_scatter | solution.py:129
  207.2 8.4 %copy-start.3 = (bf16[1,2048,1024]{2,1,0:T(8,128)(2,1)S(1)}, bf16[1,2048,1024]{2,1,0:T(8,128)(2,1)}, u32[]{:S(2)}) copy-start(bf16[1,2048,1024]{2,1,0:T(8,128)(2,1)} %all-gather.8.cloned.1.call-done) | copy-start | bytes 12582916
  207.2 12.8 %copy-start.14 = (bf16[1,128,2048]{2,1,0:T(8,128)(2,1)S(1)}, bf16[1,128,2048]{2,1,0:T(8,128)(2,1)}, u32[]{:S(2)}) copy-start(bf16[1,128,2048]{2,1,0:T(8,128)(2,1)} %constant_dynamic-slice_fusion) | copy-start | bytes 1572868
  207.2 6.7 %collective-permute-start.12 = (bf16[128,256]{1,0:T(8,128)(2,1)}, bf16[128,256]{1,0:T(8,128)(2,1)S(1)}, u32[]{:S(2)}, u32[]{:S(2)}) collective-permute-start(bf16[128,256]{1,0:T(8,128)(2,1)} %reduce-scatter.13.cloned.1.call-done), channel_id=1, source_target_pairs={{0,3},{1,0},{2,1},{3,2},{4,7},{5,4},{6,5},{7,6},{8,11},{9,8},{10,9... | collective-permute-start | bytes 196616 | tf_op jit(solution)/shard_map/ppermute | solution.py:90
  207.6 6.3 %collective-permute-start.13 = (bf16[128,256]{1,0:T(8,128)(2,1)}, bf16[128,256]{1,0:T(8,128)(2,1)S(1)}, u32[]{:S(2)}, u32[]{:S(2)}) collective-permute-start(bf16[128,256]{1,0:T(8,128)(2,1)} %reduce-scatter.13.cloned.1.call-done), channel_id=1, source_target_pairs={{0,1},{1,2},{2,3},{3,0},{4,5},{5,6},{6,7},{7,4},{8,9},{9,10},{10,1... | collective-permute-start | bytes 196616 | tf_op jit(solution)/shard_map/ppermute | solution.py:88
  213.9 6.1 %collective-permute-start.14 = (bf16[128,256]{1,0:T(8,128)(2,1)S(1)}, bf16[128,256]{1,0:T(8,128)(2,1)S(1)}, u32[]{:S(2)}, u32[]{:S(2)}) collective-permute-start(bf16[128,256]{1,0:T(8,128)(2,1)S(1)} %collective-permute-done.13), channel_id=1, source_target_pairs={{0,1},{1,2},{2,3},{3,0},{4,5},{5,6},{6,7},{7,4},{8,9},{9,10},{10,1... | collective-permute-start | bytes 196616 | tf_op jit(solution)/shard_map/ppermute | solution.py:88
  215.6 6.5 %copy-start.18 = (bf16[128,2,128]{2,1,0:T(2,128)(2,1)S(1)}, bf16[128,2,128]{2,1,0:T(2,128)(2,1)}, u32[]{:S(2)}) copy-start(bf16[128,2,128]{2,1,0:T(2,128)(2,1)} %fusion.47) | copy-start | bytes 196612
  215.6 6.8 %copy-start.20 = (bf16[128,2,128]{2,1,0:T(2,128)(2,1)S(1)}, bf16[128,2,128]{2,1,0:T(2,128)(2,1)}, u32[]{:S(2)}) copy-start(bf16[128,2,128]{2,1,0:T(2,128)(2,1)} %fusion.49) | copy-start | bytes 196612
  215.6 7.0 %copy-start.21 = (bf16[128,2,128]{2,1,0:T(2,128)(2,1)S(1)}, bf16[128,2,128]{2,1,0:T(2,128)(2,1)}, u32[]{:S(2)}) copy-start(bf16[128,2,128]{2,1,0:T(2,128)(2,1)} %fusion.51) | copy-start | bytes 196612
  220.7 12.1 %copy-start.17 = (bf16[128,2,128]{2,1,0:T(2,128)(2,1)S(1)}, bf16[128,2,128]{2,1,0:T(2,128)(2,1)}, u32[]{:S(2)}) copy-start(bf16[128,2,128]{2,1,0:T(2,128)(2,1)} %fusion.53) | copy-start | bytes 196612
  220.7 11.6 %collective-permute-start.15 = (bf16[128,2048]{1,0:T(8,128)(2,1)S(1)}, bf16[128,2048]{1,0:T(8,128)(2,1)S(1)}, u32[]{:S(2)}, u32[]{:S(2)}) collective-permute-start(bf16[128,2048]{1,0:T(8,128)(2,1)S(1)} %get-tuple-element.24), channel_id=1, source_target_pairs={{8,0},{16,8},{24,16},{9,1},{17,9},{25,17},{10,2},{18,10},{26,18},{... | collective-permute-start | bytes 1572872 | tf_op jit(solution)/shard_map/ppermute | solution.py:10
  233.6 29.5 %reduce-scatter.15.cloned.1.call-start = ((), (), s32[]{:S(2)}) async-start(), calls=%async_computation.10 | async-start | bytes 327680 | tf_op jit(solution)/shard_map/reduce_scatter | solution.py:58
  241.2 34.7 %copy-start.15 = (bf16[1,2,128,2048]{3,2,1,0:T(8,128)(2,1)S(1)}, bf16[1,2,128,2048]{3,2,1,0:T(8,128)(2,1)}, u32[]{:S(2)}) copy-start(bf16[1,2,128,2048]{3,2,1,0:T(8,128)(2,1)} %copy.135) | copy-start | bytes 3145732
  263.2 8.4 %copy-start.4 = (bf16[1,2048,1024]{2,1,0:T(8,128)(2,1)S(1)}, bf16[1,2048,1024]{2,1,0:T(8,128)(2,1)}, u32[]{:S(2)}) copy-start(bf16[1,2048,1024]{2,1,0:T(8,128)(2,1)} %all-gather.8.cloned.1.call-done) | copy-start | bytes 12582916
  263.2 6.7 %collective-permute-start.16 = (bf16[128,256]{1,0:T(8,128)(2,1)}, bf16[128,256]{1,0:T(8,128)(2,1)S(1)}, u32[]{:S(2)}, u32[]{:S(2)}) collective-permute-start(bf16[128,256]{1,0:T(8,128)(2,1)} %reduce-scatter.15.cloned.1.call-done), channel_id=1, source_target_pairs={{0,3},{1,0},{2,1},{3,2},{4,7},{5,4},{6,5},{7,6},{8,11},{9,8},{10,9... | collective-permute-start | bytes 196616 | tf_op jit(solution)/shard_map/ppermute | solution.py:90
  263.6 6.3 %collective-permute-start.17 = (bf16[128,256]{1,0:T(8,128)(2,1)}, bf16[128,256]{1,0:T(8,128)(2,1)S(1)}, u32[]{:S(2)}, u32[]{:S(2)}) collective-permute-start(bf16[128,256]{1,0:T(8,128)(2,1)} %reduce-scatter.15.cloned.1.call-done), channel_id=1, source_target_pairs={{0,1},{1,2},{2,3},{3,0},{4,5},{5,6},{6,7},{7,4},{8,9},{9,10},{10,1... | collective-permute-start | bytes 196616 | tf_op jit(solution)/shard_map/ppermute | solution.py:88
  269.9 6.1 %collective-permute-start.18 = (bf16[128,256]{1,0:T(8,128)(2,1)S(1)}, bf16[128,256]{1,0:T(8,128)(2,1)S(1)}, u32[]{:S(2)}, u32[]{:S(2)}) collective-permute-start(bf16[128,256]{1,0:T(8,128)(2,1)S(1)} %collective-permute-done.17), channel_id=1, source_target_pairs={{0,1},{1,2},{2,3},{3,0},{4,5},{5,6},{6,7},{7,4},{8,9},{9,10},{10,1... | collective-permute-start | bytes 196616 | tf_op jit(solution)/shard_map/ppermute | solution.py:88
  (4 other events, 16.7 us)
Sparse Core Ops, SparseCore 0:
  9.5 16.3 all-gather.5
  30.7 21.1 reduce-scatter.6
  53.4 11.8 all-gather.7
  93.4 19.2 reduce-scatter.8
  141.5 18.4 reduce-scatter.10
  188.7 18.4 reduce-scatter.12
  233.8 5.9 reduce-scatter.16
  242.1 21.0 reduce-scatter.14
